TPU v7x, 128 devices: a whole 4x4x4 slice. The times are simulated.
128 devices in a mesh: col: 16 (over y, x), row: 8 (over z, core).
Axes of the slice: x: 4, y: 4, z: 4, core: 2. Of those that a mesh axis runs over, the one named last changes fastest.
Arguments:
- matrix: float32 [24, 512, 8192], P(None, 'row', 'col'), may hold values from -0.4 to 2.4, as said below
- pivots: int32 [16, 512], replicated, may hold values from 0 to 511, as said below
- seeds: float32 [16, 512, 512], P('col'), may hold values from -1 to 2, as said below
Outputs:
- factors: float32 [24, 512, 8192], P(None, 'row', 'col')
Inputs may be any that keep to these rules, and one draw needn't show every extreme that they name: Each row of pivots is an ordering of 0 .. 511. Block (r, j) of matrix is zero where r and j differ by more than 8. seeds[k] approximates the inverse of block (k, k) of matrix after the replacement of rows by pivots[k].
All inputs are finite; a program needn't handle non-finite values.
Results may differ from a plain program's by a relative error of at most 0.0001.
Values sent between devices are 32-bit elements; how exact they have to be, the bound alone decides.
No kernel may reach another device: no remote copies, remote signals or barrier semaphores. Data moves between devices by JAX's collectives and lax.ppermute only.
A program may use at most 64 MiB of HBM per device.

v0:
```python
import jax
import jax.numpy as jnp
from jax import lax
from jax.sharding import PartitionSpec as P

HB = 8
SWEEPS = 2


def sent_to_all(array, axis):
    length = lax.axis_size(axis)
    return lax.all_to_all(
        jnp.broadcast_to(array[None], (length, *array.shape)), axis, 0, 0, tiled=True
    )


def in_order(parts, dim):
    lengths = list(parts.shape[1:])
    lengths[dim] *= parts.shape[0]
    return jnp.moveaxis(parts, 0, dim).reshape(lengths)


def collect(array, axis, dim):
    parts = sent_to_all(array, axis)
    return in_order(parts, dim)


def from_root(block, axis, source):
    block = jnp.where(lax.axis_index(axis) == source, block, jnp.zeros_like(block))
    return lax.psum(block, axis)


def dot_high(left, right):
    return jnp.dot(left, right, precision=lax.Precision.HIGHEST, preferred_element_type=jnp.float32)


def refine(pivot_block, approx, identity):
    for sweep_index in range(SWEEPS):
        approx = dot_high(approx, 2.0 * identity - dot_high(pivot_block, approx))
    return approx


def local(matrix, pivots, seeds):
    col_count = lax.axis_size("col")
    col_index = lax.axis_index("col")
    row_index = lax.axis_index("row")
    row_share = matrix.shape[1]
    panel_width = matrix.shape[2]
    identity = jnp.eye(panel_width, dtype=jnp.float32)
    seed_block = seeds[0]

    def eliminate(panel_index, factors):
        local_row = lax.dynamic_index_in_dim(factors, panel_index, 0, keepdims=False)
        block_row = collect(local_row, "row", 0)
        ordering = lax.dynamic_index_in_dim(pivots, panel_index, 0, keepdims=False)
        swapped = jnp.take(block_row, ordering, axis=0)
        block_row = jnp.where(col_index >= panel_index, swapped, block_row)
        local_row = lax.dynamic_slice_in_dim(block_row, row_index * row_share, row_share, 0)
        factors = lax.dynamic_update_index_in_dim(factors, local_row, panel_index, 0)
        is_owner = col_index == panel_index
        approx = lax.cond(
            is_owner, lambda: refine(block_row, seed_block, identity), lambda: seed_block
        )
        below_rows = lax.dynamic_slice_in_dim(factors, panel_index + 1, HB, 0)
        below_flat = below_rows.reshape(HB * row_share, panel_width)
        scaled = lax.cond(is_owner, lambda: dot_high(below_flat, approx), lambda: below_flat)
        in_reach = (col_index > panel_index) & (col_index <= panel_index + HB)
        arrived = from_root(scaled, "col", panel_index)
        updated = below_flat - dot_high(arrived, block_row)
        result = jnp.where(is_owner, scaled, jnp.where(in_reach, updated, below_flat))
        return lax.dynamic_update_slice_in_dim(
            factors, result.reshape(HB, row_share, panel_width), panel_index + 1, 0
        )

    return lax.fori_loop(0, col_count, eliminate, matrix)


def solution(mesh):
    return jax.shard_map(
        local,
        mesh=mesh,
        in_specs=(P(None, "row", "col"), P(), P("col", None, None)),
        out_specs=P(None, "row", "col"),
        check_vma=False,
    )
```

profile of v0, /device:TPU:0, one launch (start us, length us, event | category | flops | bytes accessed | tf_op | source)
XLA Modules:
  0.0 2143.6 jit_solution(5086388667008317163)
XLA Ops:
  10.7 2126.4 %while.17 = (s32[]{:T(128)}, f32[24,64,512]{2,1,0:T(8,128)}, s32[]{:T(128)}, s32[16,512]{1,0:T(8,128)}, s32[]{:T(128)}, /*index=5*/f32[512,512]{1,0:T(8,128)S(1)...) while((s32[]{:T(128)}, f32[24,64,512]{2,1,0:T(8,128)}, ...), condition=%wide.region_6.7_spmd.clone.clone, body=%wide.region_0.6_spmd.clone.clone.sunk | while | flops 9667090432 | bytes 55199700 | solution.py:75
  12.7 5.4 all-to-all-start
  20.0 14.0 all-to-all-done
  38.4 10.4 conditional.8
  57.5 81.4 %all-reduce.2.cloned.1.call-done = f32[512,512]{1,0:T(8,128)} async-done(((f32[512,512]{1,0:T(8,128)}), f32[512,512]{1,0:T(8,128)}) %all-reduce.2.cloned.1.call-update) | async-done | bytes 1048592 | tf_op jit(solution)/shard_map/while/body/eval_jaxpr/psum | solution.py:30
  145.4 4.4 all-to-all-start
  151.8 14.0 all-to-all-done
  174.7 96.1 %all-reduce.2.cloned.1.call-done = f32[512,512]{1,0:T(8,128)} async-done(((f32[512,512]{1,0:T(8,128)}), f32[512,512]{1,0:T(8,128)}) %all-reduce.2.cloned.1.call-update) | async-done | bytes 1048592 | tf_op jit(solution)/shard_map/while/body/eval_jaxpr/psum | solution.py:30
  277.0 4.4 all-to-all-start
  283.4 14.0 all-to-all-done
  306.3 97.1 %all-reduce.2.cloned.1.call-done = f32[512,512]{1,0:T(8,128)} async-done(((f32[512,512]{1,0:T(8,128)}), f32[512,512]{1,0:T(8,128)}) %all-reduce.2.cloned.1.call-update) | async-done | bytes 1048592 | tf_op jit(solution)/shard_map/while/body/eval_jaxpr/psum | solution.py:30
  409.6 4.4 all-to-all-start
  416.0 14.0 all-to-all-done
  438.9 97.7 %all-reduce.2.cloned.1.call-done = f32[512,512]{1,0:T(8,128)} async-done(((f32[512,512]{1,0:T(8,128)}), f32[512,512]{1,0:T(8,128)}) %all-reduce.2.cloned.1.call-update) | async-done | bytes 1048592 | tf_op jit(solution)/shard_map/while/body/eval_jaxpr/psum | solution.py:30
  542.8 4.4 all-to-all-start
  549.1 14.0 all-to-all-done
  572.1 96.4 %all-reduce.2.cloned.1.call-done = f32[512,512]{1,0:T(8,128)} async-done(((f32[512,512]{1,0:T(8,128)}), f32[512,512]{1,0:T(8,128)}) %all-reduce.2.cloned.1.call-update) | async-done | bytes 1048592 | tf_op jit(solution)/shard_map/while/body/eval_jaxpr/psum | solution.py:30
  674.6 4.4 all-to-all-start
  681.0 14.0 all-to-all-done
  703.9 96.1 %all-reduce.2.cloned.1.call-done = f32[512,512]{1,0:T(8,128)} async-done(((f32[512,512]{1,0:T(8,128)}), f32[512,512]{1,0:T(8,128)}) %all-reduce.2.cloned.1.call-update) | async-done | bytes 1048592 | tf_op jit(solution)/shard_map/while/body/eval_jaxpr/psum | solution.py:30
  806.2 4.4 all-to-all-start
  812.6 14.0 all-to-all-done
  835.5 97.3 %all-reduce.2.cloned.1.call-done = f32[512,512]{1,0:T(8,128)} async-done(((f32[512,512]{1,0:T(8,128)}), f32[512,512]{1,0:T(8,128)}) %all-reduce.2.cloned.1.call-update) | async-done | bytes 1048592 | tf_op jit(solution)/shard_map/while/body/eval_jaxpr/psum | solution.py:30
  939.0 4.4 all-to-all-start
  945.4 14.0 all-to-all-done
  968.3 97.3 %all-reduce.2.cloned.1.call-done = f32[512,512]{1,0:T(8,128)} async-done(((f32[512,512]{1,0:T(8,128)}), f32[512,512]{1,0:T(8,128)}) %all-reduce.2.cloned.1.call-update) | async-done | bytes 1048592 | tf_op jit(solution)/shard_map/while/body/eval_jaxpr/psum | solution.py:30
  1071.8 4.4 all-to-all-start
  1078.2 14.0 all-to-all-done
  1101.1 97.0 %all-reduce.2.cloned.1.call-done = f32[512,512]{1,0:T(8,128)} async-done(((f32[512,512]{1,0:T(8,128)}), f32[512,512]{1,0:T(8,128)}) %all-reduce.2.cloned.1.call-update) | async-done | bytes 1048592 | tf_op jit(solution)/shard_map/while/body/eval_jaxpr/psum | solution.py:30
  1204.3 4.4 all-to-all-start
  1210.7 14.0 all-to-all-done
  1233.6 97.5 %all-reduce.2.cloned.1.call-done = f32[512,512]{1,0:T(8,128)} async-done(((f32[512,512]{1,0:T(8,128)}), f32[512,512]{1,0:T(8,128)}) %all-reduce.2.cloned.1.call-update) | async-done | bytes 1048592 | tf_op jit(solution)/shard_map/while/body/eval_jaxpr/psum | solution.py:30
  1337.2 4.4 all-to-all-start
  1343.6 14.0 all-to-all-done
  1366.5 98.8 %all-reduce.2.cloned.1.call-done = f32[512,512]{1,0:T(8,128)} async-done(((f32[512,512]{1,0:T(8,128)}), f32[512,512]{1,0:T(8,128)}) %all-reduce.2.cloned.1.call-update) | async-done | bytes 1048592 | tf_op jit(solution)/shard_map/while/body/eval_jaxpr/psum | solution.py:30
  1471.5 4.4 all-to-all-start
  1477.9 14.0 all-to-all-done
  1500.8 98.6 %all-reduce.2.cloned.1.call-done = f32[512,512]{1,0:T(8,128)} async-done(((f32[512,512]{1,0:T(8,128)}), f32[512,512]{1,0:T(8,128)}) %all-reduce.2.cloned.1.call-update) | async-done | bytes 1048592 | tf_op jit(solution)/shard_map/while/body/eval_jaxpr/psum | solution.py:30
  1605.6 4.4 all-to-all-start
  1612.0 14.0 all-to-all-done
  1634.9 97.6 %all-reduce.2.cloned.1.call-done = f32[512,512]{1,0:T(8,128)} async-done(((f32[512,512]{1,0:T(8,128)}), f32[512,512]{1,0:T(8,128)}) %all-reduce.2.cloned.1.call-update) | async-done | bytes 1048592 | tf_op jit(solution)/shard_map/while/body/eval_jaxpr/psum | solution.py:30
  1745.1 14.0 all-to-all-done
  1768.0 97.2 %all-reduce.2.cloned.1.call-done = f32[512,512]{1,0:T(8,128)} async-done(((f32[512,512]{1,0:T(8,128)}), f32[512,512]{1,0:T(8,128)}) %all-reduce.2.cloned.1.call-update) | async-done | bytes 1048592 | tf_op jit(solution)/shard_map/while/body/eval_jaxpr/psum | solution.py:30
  1871.4 4.4 all-to-all-start
  1877.8 14.0 all-to-all-done
  1900.7 98.6 %all-reduce.2.cloned.1.call-done = f32[512,512]{1,0:T(8,128)} async-done(((f32[512,512]{1,0:T(8,128)}), f32[512,512]{1,0:T(8,128)}) %all-reduce.2.cloned.1.call-update) | async-done | bytes 1048592 | tf_op jit(solution)/shard_map/while/body/eval_jaxpr/psum | solution.py:30
  2011.8 14.0 all-to-all-done
  2034.8 98.2 %all-reduce.2.cloned.1.call-done = f32[512,512]{1,0:T(8,128)} async-done(((f32[512,512]{1,0:T(8,128)}), f32[512,512]{1,0:T(8,128)}) %all-reduce.2.cloned.1.call-update) | async-done | bytes 1048592 | tf_op jit(solution)/shard_map/while/body/eval_jaxpr/psum | solution.py:30
  (345 shorter events, 318.5 us)
Async XLA Ops:
  6.5 4.1 copy-start
  12.7 21.4 all-to-all-start
  18.1 120.9 %all-reduce.2.cloned.1.call-start = ((), (), s32[]{:S(2)}) async-start(), calls=%async_computation.1 | async-start | bytes 2097152 | tf_op jit(solution)/shard_map/while/body/eval_jaxpr/psum | solution.py:30
  38.4 6.7 copy-start.1
  48.8 1.0 copy-start.2
  145.4 20.4 all-to-all-start
  149.9 121.0 %all-reduce.2.cloned.1.call-start = ((), (), s32[]{:S(2)}) async-start(), calls=%async_computation.1 | async-start | bytes 2097152 | tf_op jit(solution)/shard_map/while/body/eval_jaxpr/psum | solution.py:30
  170.3 1.0 copy-start.2
  277.0 20.4 all-to-all-start
  281.4 122.0 %all-reduce.2.cloned.1.call-start = ((), (), s32[]{:S(2)}) async-start(), calls=%async_computation.1 | async-start | bytes 2097152 | tf_op jit(solution)/shard_map/while/body/eval_jaxpr/psum | solution.py:30
  301.9 1.0 copy-start.2
  409.6 20.4 all-to-all-start
  414.1 122.5 %all-reduce.2.cloned.1.call-start = ((), (), s32[]{:S(2)}) async-start(), calls=%async_computation.1 | async-start | bytes 2097152 | tf_op jit(solution)/shard_map/while/body/eval_jaxpr/psum | solution.py:30
  434.5 1.0 copy-start.2
  542.8 20.4 all-to-all-start
  547.2 121.3 %all-reduce.2.cloned.1.call-start = ((), (), s32[]{:S(2)}) async-start(), calls=%async_computation.1 | async-start | bytes 2097152 | tf_op jit(solution)/shard_map/while/body/eval_jaxpr/psum | solution.py:30
  567.6 1.0 copy-start.2
  674.6 20.4 all-to-all-start
  679.1 121.0 %all-reduce.2.cloned.1.call-start = ((), (), s32[]{:S(2)}) async-start(), calls=%async_computation.1 | async-start | bytes 2097152 | tf_op jit(solution)/shard_map/while/body/eval_jaxpr/psum | solution.py:30
  699.5 1.0 copy-start.2
  806.2 20.4 all-to-all-start
  810.7 122.2 %all-reduce.2.cloned.1.call-start = ((), (), s32[]{:S(2)}) async-start(), calls=%async_computation.1 | async-start | bytes 2097152 | tf_op jit(solution)/shard_map/while/body/eval_jaxpr/psum | solution.py:30
  831.1 1.0 copy-start.2
  939.0 20.4 all-to-all-start
  943.5 122.2 %all-reduce.2.cloned.1.call-start = ((), (), s32[]{:S(2)}) async-start(), calls=%async_computation.1 | async-start | bytes 2097152 | tf_op jit(solution)/shard_map/while/body/eval_jaxpr/psum | solution.py:30
  963.9 1.0 copy-start.2
  1071.8 20.4 all-to-all-start
  1076.3 121.9 %all-reduce.2.cloned.1.call-start = ((), (), s32[]{:S(2)}) async-start(), calls=%async_computation.1 | async-start | bytes 2097152 | tf_op jit(solution)/shard_map/while/body/eval_jaxpr/psum | solution.py:30
  1096.7 1.0 copy-start.2
  1204.3 20.4 all-to-all-start
  1208.7 122.3 %all-reduce.2.cloned.1.call-start = ((), (), s32[]{:S(2)}) async-start(), calls=%async_computation.1 | async-start | bytes 2097152 | tf_op jit(solution)/shard_map/while/body/eval_jaxpr/psum | solution.py:30
  1229.2 1.0 copy-start.2
  1337.2 20.4 all-to-all-start
  1341.7 123.7 %all-reduce.2.cloned.1.call-start = ((), (), s32[]{:S(2)}) async-start(), calls=%async_computation.1 | async-start | bytes 2097152 | tf_op jit(solution)/shard_map/while/body/eval_jaxpr/psum | solution.py:30
  1362.1 1.0 copy-start.2
  1471.5 20.4 all-to-all-start
  1476.0 123.4 %all-reduce.2.cloned.1.call-start = ((), (), s32[]{:S(2)}) async-start(), calls=%async_computation.1 | async-start | bytes 2097152 | tf_op jit(solution)/shard_map/while/body/eval_jaxpr/psum | solution.py:30
  1496.4 1.0 copy-start.2
  1605.6 20.4 all-to-all-start
  1610.0 122.5 %all-reduce.2.cloned.1.call-start = ((), (), s32[]{:S(2)}) async-start(), calls=%async_computation.1 | async-start | bytes 2097152 | tf_op jit(solution)/shard_map/while/body/eval_jaxpr/psum | solution.py:30
  1630.5 1.0 copy-start.2
  1738.7 20.4 all-to-all-start
  1743.1 122.1 %all-reduce.2.cloned.1.call-start = ((), (), s32[]{:S(2)}) async-start(), calls=%async_computation.1 | async-start | bytes 2097152 | tf_op jit(solution)/shard_map/while/body/eval_jaxpr/psum | solution.py:30
  1871.4 20.4 all-to-all-start
  1875.8 123.5 %all-reduce.2.cloned.1.call-start = ((), (), s32[]{:S(2)}) async-start(), calls=%async_computation.1 | async-start | bytes 2097152 | tf_op jit(solution)/shard_map/while/body/eval_jaxpr/psum | solution.py:30
  2005.5 20.4 all-to-all-start
  2009.9 123.0 %all-reduce.2.cloned.1.call-start = ((), (), s32[]{:S(2)}) async-start(), calls=%async_computation.1 | async-start | bytes 2097152 | tf_op jit(solution)/shard_map/while/body/eval_jaxpr/psum | solution.py:30
  2030.3 1.0 copy-start.2
  (2 other events, 1.9 us)
Sparse Core Ops, SparseCore 0:
  57.6 81.2 all-reduce.1
  174.8 95.9 all-reduce.1
  306.4 96.9 all-reduce.1
  439.0 97.4 all-reduce.1
  572.2 96.2 all-reduce.1
  704.1 95.9 all-reduce.1
  835.6 97.1 all-reduce.1
  968.5 97.1 all-reduce.1
  1101.2 96.8 all-reduce.1
  1233.7 97.2 all-reduce.1
  1366.6 98.6 all-reduce.1
  1501.0 98.4 all-reduce.1
  1635.0 97.4 all-reduce.1
  1768.1 97.0 all-reduce.1
  1900.8 98.4 all-reduce.1
  2034.9 97.9 all-reduce.1
where the time goes:
time: 2150 us; the launch traced here: 2140 us
  waiting for transfers between devices  1770 us (82%)
  local copies, waits for them, and re-layouts  153 us (7%)
  starting transfers between devices  72.4 us (3%)
  other arithmetic  70.8 us (3%)
  matrix products  64.5 us (3%)
    psum x16, waiting for transfers between devices, from_root(): return lax.psum(block, axis)  1540 us
    all_to_all x16, waiting for transfers between devices, sent_to_all(): lax.all_to_all(jnp.broadcast_to(array[None], (length, *array.shape)), axi...  225 us
    all_to_all x16, starting transfers between devices, sent_to_all(): lax.all_to_all(jnp.broadcast_to(array[None], (length, *array.shape)), axi...  71.8 us
    dot_general x21, matrix products, dot_high(): jnp.dot(left, right, precision=lax.Precision.HIGHEST, preferred_element_t...  64.5 us
  transfers between devices with their start and end apart: 32, of which 32 were waited for; matrix products, arithmetic and copies ran while one was open for 1% of the time, Pallas kernels for 0%

commit v1 on v0

--- a/solution.py
+++ b/solution.py
@@ -2,6 +2,7 @@
 import jax.numpy as jnp
 from jax import lax
 from jax.sharding import PartitionSpec as P
+from jax.lax import all_gather
 
 HB = 8
 SWEEPS = 2
@@ -27,7 +28,8 @@
 
 def from_root(block, axis, source):
     block = jnp.where(lax.axis_index(axis) == source, block, jnp.zeros_like(block))
-    return lax.psum(block, axis)
+    work_the_links = lambda state, along_axis: all_gather(state, along_axis).sum(axis=0)
+    return work_the_links(block, axis)
 
 
 def dot_high(left, right):

time: 2150 us -> 2690 us (1.25)
  waiting for transfers between devices: 1770 us -> 2170 us
  other arithmetic: 70.8 us -> 213 us
    all_gather x0 -> x16, waiting for transfers between devices: none -> 1940 us  [from_root(): all_gather(state, along_axis).sum(axis=0)]
    psum x16 -> x0, waiting for transfers between devices: 1540 us -> none  [from_root(): return lax.psum(block, axis)]
    reduce_sum x0 -> x16, other arithmetic: none -> 142 us  [from_root(): all_gather(state, along_axis).sum(axis=0)]
where the time goes in v1:
time: 2690 us; the launch traced here: 2680 us
  waiting for transfers between devices  2170 us (81%)
  other arithmetic  213 us (8%)
  local copies, waits for them, and re-layouts  153 us (6%)
  starting transfers between devices  72.3 us (3%)
  matrix products  64.5 us (2%)
    all_gather x16, waiting for transfers between devices, from_root(): all_gather(state, along_axis).sum(axis=0)  1940 us
    all_to_all x16, waiting for transfers between devices, sent_to_all(): lax.all_to_all(jnp.broadcast_to(array[None], (length, *array.shape)), axi...  225 us
    reduce_sum x16, other arithmetic, from_root(): all_gather(state, along_axis).sum(axis=0)  142 us
    all_to_all x16, starting transfers between devices, sent_to_all(): lax.all_to_all(jnp.broadcast_to(array[None], (length, *array.shape)), axi...  71.8 us
    dot_general x21, matrix products, dot_high(): jnp.dot(left, right, precision=lax.Precision.HIGHEST, preferred_element_t...  64.5 us
  transfers between devices with their start and end apart: 32, of which 32 were waited for; matrix products, arithmetic and copies ran while one was open for 1% of the time, Pallas kernels for 0%

profile of v1, /device:TPU:0, one launch (start us, length us, event | category | flops | bytes accessed | tf_op | source)
XLA Modules:
  0.0 2684.5 jit_solution(3608957134663954694)
XLA Ops:
  10.7 2667.3 %while.17 = (s32[]{:T(128)}, f32[24,64,512]{2,1,0:T(8,128)}, s32[]{:T(128)}, s32[16,512]{1,0:T(8,128)}, s32[]{:T(128)}, /*index=5*/f32[512,512]{1,0:T(8,128)S(1)...) while((s32[]{:T(128)}, f32[24,64,512]{2,1,0:T(8,128)}, ...), condition=%wide.region_6.7_spmd.clone.clone, body=%wide.region_0.6_spmd.clone.clone.sunk | while | flops 9670760448 | bytes 120211424 | solution.py:77
  20.0 14.0 all-to-all-done
  38.4 10.4 conditional.8
  57.5 105.8 %all-gather.6.cloned.1.call-done = f32[8192,512]{1,0:T(8,128)} async-done(((f32[512,512]{1,0:T(8,128)}), f32[8192,512]{1,0:T(8,128)}) %all-gather.6.cloned.1.call-update) | async-done | bytes 16777232 | tf_op jit(solution)/shard_map/while/body/eval_jaxpr/all_gather | solution.py:31
  163.3 8.9 reduce_sum.19
  185.0 14.0 all-to-all-done
  208.0 120.9 %all-gather.6.cloned.1.call-done = f32[8192,512]{1,0:T(8,128)} async-done(((f32[512,512]{1,0:T(8,128)}), f32[8192,512]{1,0:T(8,128)}) %all-gather.6.cloned.1.call-update) | async-done | bytes 16777232 | tf_op jit(solution)/shard_map/while/body/eval_jaxpr/all_gather | solution.py:31
  328.9 8.9 reduce_sum.19
  350.3 14.0 all-to-all-done
  373.2 122.7 %all-gather.6.cloned.1.call-done = f32[8192,512]{1,0:T(8,128)} async-done(((f32[512,512]{1,0:T(8,128)}), f32[8192,512]{1,0:T(8,128)}) %all-gather.6.cloned.1.call-update) | async-done | bytes 16777232 | tf_op jit(solution)/shard_map/while/body/eval_jaxpr/all_gather | solution.py:31
  496.0 8.9 reduce_sum.19
  517.4 14.0 all-to-all-done
  540.3 122.4 %all-gather.6.cloned.1.call-done = f32[8192,512]{1,0:T(8,128)} async-done(((f32[512,512]{1,0:T(8,128)}), f32[8192,512]{1,0:T(8,128)}) %all-gather.6.cloned.1.call-update) | async-done | bytes 16777232 | tf_op jit(solution)/shard_map/while/body/eval_jaxpr/all_gather | solution.py:31
  662.8 8.9 reduce_sum.19
  684.2 14.0 all-to-all-done
  707.1 121.2 %all-gather.6.cloned.1.call-done = f32[8192,512]{1,0:T(8,128)} async-done(((f32[512,512]{1,0:T(8,128)}), f32[8192,512]{1,0:T(8,128)}) %all-gather.6.cloned.1.call-update) | async-done | bytes 16777232 | tf_op jit(solution)/shard_map/while/body/eval_jaxpr/all_gather | solution.py:31
  828.4 8.9 reduce_sum.19
  849.8 14.0 all-to-all-done
  872.7 120.9 %all-gather.6.cloned.1.call-done = f32[8192,512]{1,0:T(8,128)} async-done(((f32[512,512]{1,0:T(8,128)}), f32[8192,512]{1,0:T(8,128)}) %all-gather.6.cloned.1.call-update) | async-done | bytes 16777232 | tf_op jit(solution)/shard_map/while/body/eval_jaxpr/all_gather | solution.py:31
  993.7 8.9 reduce_sum.19
  1015.1 14.0 all-to-all-done
  1038.0 122.4 %all-gather.6.cloned.1.call-done = f32[8192,512]{1,0:T(8,128)} async-done(((f32[512,512]{1,0:T(8,128)}), f32[8192,512]{1,0:T(8,128)}) %all-gather.6.cloned.1.call-update) | async-done | bytes 16777232 | tf_op jit(solution)/shard_map/while/body/eval_jaxpr/all_gather | solution.py:31
  1160.5 8.9 reduce_sum.19
  1181.9 14.0 all-to-all-done
  1204.8 122.2 %all-gather.6.cloned.1.call-done = f32[8192,512]{1,0:T(8,128)} async-done(((f32[512,512]{1,0:T(8,128)}), f32[8192,512]{1,0:T(8,128)}) %all-gather.6.cloned.1.call-update) | async-done | bytes 16777232 | tf_op jit(solution)/shard_map/while/body/eval_jaxpr/all_gather | solution.py:31
  1327.0 8.9 reduce_sum.19
  1348.4 14.0 all-to-all-done
  1371.3 122.8 %all-gather.6.cloned.1.call-done = f32[8192,512]{1,0:T(8,128)} async-done(((f32[512,512]{1,0:T(8,128)}), f32[8192,512]{1,0:T(8,128)}) %all-gather.6.cloned.1.call-update) | async-done | bytes 16777232 | tf_op jit(solution)/shard_map/while/body/eval_jaxpr/all_gather | solution.py:31
  1494.1 8.9 reduce_sum.19
  1515.5 14.0 all-to-all-done
  1538.4 122.4 %all-gather.6.cloned.1.call-done = f32[8192,512]{1,0:T(8,128)} async-done(((f32[512,512]{1,0:T(8,128)}), f32[8192,512]{1,0:T(8,128)}) %all-gather.6.cloned.1.call-update) | async-done | bytes 16777232 | tf_op jit(solution)/shard_map/while/body/eval_jaxpr/all_gather | solution.py:31
  1660.9 8.9 reduce_sum.19
  1682.3 14.0 all-to-all-done
  1705.2 123.7 %all-gather.6.cloned.1.call-done = f32[8192,512]{1,0:T(8,128)} async-done(((f32[512,512]{1,0:T(8,128)}), f32[8192,512]{1,0:T(8,128)}) %all-gather.6.cloned.1.call-update) | async-done | bytes 16777232 | tf_op jit(solution)/shard_map/while/body/eval_jaxpr/all_gather | solution.py:31
  1828.9 8.9 reduce_sum.19
  1850.3 14.0 all-to-all-done
  1873.3 123.4 %all-gather.6.cloned.1.call-done = f32[8192,512]{1,0:T(8,128)} async-done(((f32[512,512]{1,0:T(8,128)}), f32[8192,512]{1,0:T(8,128)}) %all-gather.6.cloned.1.call-update) | async-done | bytes 16777232 | tf_op jit(solution)/shard_map/while/body/eval_jaxpr/all_gather | solution.py:31
  1996.7 8.9 reduce_sum.19
  2018.1 14.0 all-to-all-done
  2041.0 122.5 %all-gather.6.cloned.1.call-done = f32[8192,512]{1,0:T(8,128)} async-done(((f32[512,512]{1,0:T(8,128)}), f32[8192,512]{1,0:T(8,128)}) %all-gather.6.cloned.1.call-update) | async-done | bytes 16777232 | tf_op jit(solution)/shard_map/while/body/eval_jaxpr/all_gather | solution.py:31
  2184.9 14.0 all-to-all-done
  2207.9 122.2 %all-gather.6.cloned.1.call-done = f32[8192,512]{1,0:T(8,128)} async-done(((f32[512,512]{1,0:T(8,128)}), f32[8192,512]{1,0:T(8,128)}) %all-gather.6.cloned.1.call-update) | async-done | bytes 16777232 | tf_op jit(solution)/shard_map/while/body/eval_jaxpr/all_gather | solution.py:31
  2330.0 8.9 reduce_sum.19
  2351.5 14.0 all-to-all-done
  2374.4 123.4 %all-gather.6.cloned.1.call-done = f32[8192,512]{1,0:T(8,128)} async-done(((f32[512,512]{1,0:T(8,128)}), f32[8192,512]{1,0:T(8,128)}) %all-gather.6.cloned.1.call-update) | async-done | bytes 16777232 | tf_op jit(solution)/shard_map/while/body/eval_jaxpr/all_gather | solution.py:31
  2497.8 8.9 reduce_sum.19
  2519.2 14.0 all-to-all-done
  2542.1 122.8 %all-gather.6.cloned.1.call-done = f32[8192,512]{1,0:T(8,128)} async-done(((f32[512,512]{1,0:T(8,128)}), f32[8192,512]{1,0:T(8,128)}) %all-gather.6.cloned.1.call-update) | async-done | bytes 16777232 | tf_op jit(solution)/shard_map/while/body/eval_jaxpr/all_gather | solution.py:31
  (361 shorter events, 399.3 us)
Async XLA Ops:
  6.5 4.1 copy-start
  12.7 21.4 all-to-all-start
  18.1 145.2 %all-gather.6.cloned.1.call-start = ((), (), s32[]{:S(2)}) async-start(), calls=%async_computation.1 | async-start | bytes 17825792 | tf_op jit(solution)/shard_map/while/body/eval_jaxpr/all_gather | solution.py:31
  38.4 6.7 copy-start.1
  48.8 1.0 copy-start.2
  178.7 20.4 all-to-all-start
  183.1 145.8 %all-gather.6.cloned.1.call-start = ((), (), s32[]{:S(2)}) async-start(), calls=%async_computation.1 | async-start | bytes 17825792 | tf_op jit(solution)/shard_map/while/body/eval_jaxpr/all_gather | solution.py:31
  203.5 1.0 copy-start.2
  344.0 20.4 all-to-all-start
  348.4 147.6 %all-gather.6.cloned.1.call-start = ((), (), s32[]{:S(2)}) async-start(), calls=%async_computation.1 | async-start | bytes 17825792 | tf_op jit(solution)/shard_map/while/body/eval_jaxpr/all_gather | solution.py:31
  368.8 1.0 copy-start.2
  511.0 20.4 all-to-all-start
  515.5 147.3 %all-gather.6.cloned.1.call-start = ((), (), s32[]{:S(2)}) async-start(), calls=%async_computation.1 | async-start | bytes 17825792 | tf_op jit(solution)/shard_map/while/body/eval_jaxpr/all_gather | solution.py:31
  535.9 1.0 copy-start.2
  677.9 20.4 all-to-all-start
  682.3 146.1 %all-gather.6.cloned.1.call-start = ((), (), s32[]{:S(2)}) async-start(), calls=%async_computation.1 | async-start | bytes 17825792 | tf_op jit(solution)/shard_map/while/body/eval_jaxpr/all_gather | solution.py:31
  702.7 1.0 copy-start.2
  843.4 20.4 all-to-all-start
  847.9 145.8 %all-gather.6.cloned.1.call-start = ((), (), s32[]{:S(2)}) async-start(), calls=%async_computation.1 | async-start | bytes 17825792 | tf_op jit(solution)/shard_map/while/body/eval_jaxpr/all_gather | solution.py:31
  868.3 1.0 copy-start.2
  1008.7 20.4 all-to-all-start
  1013.2 147.3 %all-gather.6.cloned.1.call-start = ((), (), s32[]{:S(2)}) async-start(), calls=%async_computation.1 | async-start | bytes 17825792 | tf_op jit(solution)/shard_map/while/body/eval_jaxpr/all_gather | solution.py:31
  1033.6 1.0 copy-start.2
  1175.5 20.4 all-to-all-start
  1180.0 147.0 %all-gather.6.cloned.1.call-start = ((), (), s32[]{:S(2)}) async-start(), calls=%async_computation.1 | async-start | bytes 17825792 | tf_op jit(solution)/shard_map/while/body/eval_jaxpr/all_gather | solution.py:31
  1200.4 1.0 copy-start.2
  1342.0 20.4 all-to-all-start
  1346.5 147.6 %all-gather.6.cloned.1.call-start = ((), (), s32[]{:S(2)}) async-start(), calls=%async_computation.1 | async-start | bytes 17825792 | tf_op jit(solution)/shard_map/while/body/eval_jaxpr/all_gather | solution.py:31
  1366.9 1.0 copy-start.2
  1509.2 20.4 all-to-all-start
  1513.6 147.3 %all-gather.6.cloned.1.call-start = ((), (), s32[]{:S(2)}) async-start(), calls=%async_computation.1 | async-start | bytes 17825792 | tf_op jit(solution)/shard_map/while/body/eval_jaxpr/all_gather | solution.py:31
  1675.9 20.4 all-to-all-start
  1680.4 148.5 %all-gather.6.cloned.1.call-start = ((), (), s32[]{:S(2)}) async-start(), calls=%async_computation.1 | async-start | bytes 17825792 | tf_op jit(solution)/shard_map/while/body/eval_jaxpr/all_gather | solution.py:31
  1700.8 1.0 copy-start.2
  1844.0 20.4 all-to-all-start
  1848.4 148.3 %all-gather.6.cloned.1.call-start = ((), (), s32[]{:S(2)}) async-start(), calls=%async_computation.1 | async-start | bytes 17825792 | tf_op jit(solution)/shard_map/while/body/eval_jaxpr/all_gather | solution.py:31
  1868.8 1.0 copy-start.2
  2011.7 20.4 all-to-all-start
  2016.2 147.3 %all-gather.6.cloned.1.call-start = ((), (), s32[]{:S(2)}) async-start(), calls=%async_computation.1 | async-start | bytes 17825792 | tf_op jit(solution)/shard_map/while/body/eval_jaxpr/all_gather | solution.py:31
  2036.6 1.0 copy-start.2
  2178.6 20.4 all-to-all-start
  2183.0 147.0 %all-gather.6.cloned.1.call-start = ((), (), s32[]{:S(2)}) async-start(), calls=%async_computation.1 | async-start | bytes 17825792 | tf_op jit(solution)/shard_map/while/body/eval_jaxpr/all_gather | solution.py:31
  2203.4 1.0 copy-start.2
  2345.1 20.4 all-to-all-start
  2349.5 148.2 %all-gather.6.cloned.1.call-start = ((), (), s32[]{:S(2)}) async-start(), calls=%async_computation.1 | async-start | bytes 17825792 | tf_op jit(solution)/shard_map/while/body/eval_jaxpr/all_gather | solution.py:31
  2370.0 1.0 copy-start.2
  2512.8 20.4 all-to-all-start
  2517.3 147.6 %all-gather.6.cloned.1.call-start = ((), (), s32[]{:S(2)}) async-start(), calls=%async_computation.1 | async-start | bytes 17825792 | tf_op jit(solution)/shard_map/while/body/eval_jaxpr/all_gather | solution.py:31
  (2 other events, 1.9 us)
Sparse Core Ops, SparseCore 0:
  57.6 105.6 all-gather.5
  208.1 120.7 all-gather.5
  373.4 122.5 all-gather.5
  540.4 122.2 all-gather.5
  707.3 121.0 all-gather.5
  872.8 120.7 all-gather.5
  1038.1 122.2 all-gather.5
  1204.9 121.9 all-gather.5
  1371.4 122.5 all-gather.5
  1538.6 122.2 all-gather.5
  1705.3 123.5 all-gather.5
  1873.4 123.2 all-gather.5
  2041.1 122.3 all-gather.5
  2208.0 122.0 all-gather.5
  2374.5 123.2 all-gather.5
  2542.2 122.6 all-gather.5
